TPU v7x, 32 devices: a whole 2x2x4 slice. The times are simulated.
32 devices in a mesh: section: 4 (over z), tensor: 8 (over y, x, core).
Axes of the slice: x: 2, y: 2, z: 4, core: 2. Of those that a mesh axis runs over, the one named last changes fastest.
Arguments:
- activations: bfloat16 [4, 8192, 128], P('section', 'tensor'), may hold values from -6 to 6
- out_grads: bfloat16 [4, 8192, 128], P('section', 'tensor'), may hold values from -1.5 to 1.5
- w_in: bfloat16 [4, 256, 6, 128, 128], P('section', 'tensor'), may hold values from -0.25 to 0.25
- w_out: bfloat16 [4, 256, 6, 128, 128], P('section', 'tensor'), may hold values from -0.25 to 0.25
- bias_in: bfloat16 [4, 32768], P('section', 'tensor'), may hold values from -3 to 3
- cols_in: int32 [4, 256, 6], P('section', 'tensor'), may hold values from 0 to 63, as said below
- mask_in: int32 [4, 256, 6], P('section', 'tensor'), may hold values from 0 to 1, as said below
- cols_out: int32 [4, 256, 6], P('section', 'tensor'), may hold values from 0 to 63, as said below
- mask_out: int32 [4, 256, 6], P('section', 'tensor'), may hold values from 0 to 1, as said below
- block_rows: int32 [4, 256], P('section', 'tensor'), may hold values from 0 to 255, each once within a row
Outputs:
- grad_w_in: bfloat16 [4, 256, 6, 128, 128], P('section', 'tensor')
- grad_w_out: bfloat16 [4, 256, 6, 128, 128], P('section', 'tensor')
- grad_bias: float32 [4, 32768], P('section', 'tensor')
- handed: bfloat16 [4, 8192, 128], P('section', 'tensor')
Inputs may be any that keep to these rules, and one draw needn't show every extreme that they name: `cols_in`: in each stored row the 6 entries are distinct feature blocks; only slots with mask_in 1 are used. `mask_in`: each stored row has its valid slots first: 1 on the first 2 to 6 slots, 0 after; some row of every draw has all 6 slots valid. `cols_out`: in each stored row the 6 entries are distinct feature blocks; only slots with mask_out 1 are used. `mask_out`: each stored row has its valid slots first: 1 on the first 2 to 6 slots, 0 after; some row of every draw has all 6 slots valid. `block_rows`: for each section, a permutation of the 256 hidden blocks.
All inputs are finite; a program needn't handle non-finite values.
Results may differ from a plain program's by a relative error of at most 0.0049.
Values may be sent and summed in bfloat16 or wider, within the bound.
A program may use at most 128 MiB of HBM per device.

v0:
```python
import jax
import jax.numpy as jnp
from jax import lax
from jax.sharding import PartitionSpec as P

D = 8192
FF = 32768
BLK = 128
TOK = 128
DBLOCKS = 64
HBLOCKS = 256


def from_behind(shard, axis, by):
    devices = lax.axis_size(axis)
    return lax.ppermute(shard, axis, [(i, (i + by) % devices) for i in range(devices)])


def gelu_parts(pre_act):
    cdf_part = 0.5 * (1.0 + jax.scipy.special.erf(pre_act * 0.7071067811865476))
    density = jnp.exp(-0.5 * pre_act * pre_act) * 0.3989422804014327
    return (pre_act * cdf_part, cdf_part + pre_act * density)


def local(
    activations, out_grads, w_in, w_out, bias_in, cols_in, mask_in, cols_out, mask_out, block_rows
):
    act_all, grad_all, bias_all = (
        lax.all_gather(activations, "tensor", axis=1, tiled=True),
        lax.all_gather(out_grads, "tensor", axis=1, tiled=True),
        lax.all_gather(bias_in, "tensor", axis=1, tiled=True),
    )
    act_blocks = act_all[0].reshape(DBLOCKS, BLK, TOK)
    grad_blocks = grad_all[0].reshape(DBLOCKS, BLK, TOK)
    bias_blocks = bias_all[0].reshape(HBLOCKS, BLK)
    stored = block_rows[0]
    col_in = cols_in[0]
    col_out = cols_out[0]
    valid_in = mask_in[0]
    valid_out = mask_out[0]
    select = stored[:, None] == jnp.arange(HBLOCKS, dtype=jnp.int32)[None, :]
    bias_rows = jnp.dot(
        select.astype(jnp.bfloat16), bias_blocks, preferred_element_type=jnp.float32
    )
    zero_grad = jnp.zeros((DBLOCKS, BLK, TOK), jnp.float32)
    w_keep_in = jnp.where((valid_in > 0)[:, :, None, None], w_in[0], jnp.zeros_like(w_in[0]))
    w_keep_out = jnp.where((valid_out > 0)[:, :, None, None], w_out[0], jnp.zeros_like(w_out[0]))
    slots_act = act_blocks[col_in]
    slots_grad = grad_blocks[col_out]
    pre_act = (
        jnp.einsum("rsij,rsjt->rit", w_keep_in, slots_act, preferred_element_type=jnp.float32)
        + bias_rows[:, :, None]
    )
    act_value, gelu_slope = gelu_parts(pre_act)
    hidden = act_value.astype(jnp.bfloat16)
    grad_hidden = jnp.einsum(
        "rsij,rsjt->rit", w_keep_out, slots_grad, preferred_element_type=jnp.float32
    )
    grad_pre = grad_hidden * gelu_slope
    grad_low = grad_pre.astype(jnp.bfloat16)
    tiles_out = jnp.einsum("rit,rsjt->rsij", hidden, slots_grad, preferred_element_type=jnp.float32)
    tiles_out = jnp.where((valid_out > 0)[:, :, None, None], tiles_out, 0.0).astype(jnp.bfloat16)
    tiles_in = jnp.einsum("rit,rsjt->rsij", grad_low, slots_act, preferred_element_type=jnp.float32)
    tiles_in = jnp.where((valid_in > 0)[:, :, None, None], tiles_in, 0.0).astype(jnp.bfloat16)
    pieces = jnp.einsum("rsij,rit->rsjt", w_keep_in, grad_low, preferred_element_type=jnp.float32)
    input_grad = zero_grad.at[col_in.reshape(-1)].add(pieces.reshape(-1, BLK, TOK))
    bias_grad = jnp.sum(grad_pre, axis=2)
    bias_full = jnp.einsum(
        "rh,rb->hb", select.astype(jnp.float32), bias_grad, precision=lax.Precision.HIGHEST
    )
    bias_full = bias_full.reshape(1, FF)
    input_terms = input_grad.reshape(1, D, TOK)
    grad_sum, bias_sum = (
        lax.psum_scatter(input_terms, "tensor", scatter_dimension=1, tiled=True),
        lax.psum_scatter(bias_full, "tensor", scatter_dimension=1, tiled=True),
    )
    handed = from_behind(grad_sum.astype(jnp.bfloat16), "section", -1)
    return (tiles_in[None], tiles_out[None], bias_sum, handed)


def solution(mesh):
    return jax.shard_map(
        local,
        mesh=mesh,
        in_specs=(
            P("section", "tensor", None),
            P("section", "tensor", None),
            P("section", "tensor", None, None, None),
            P("section", "tensor", None, None, None),
            P("section", "tensor"),
            P("section", "tensor", None),
            P("section", "tensor", None),
            P("section", "tensor", None),
            P("section", "tensor", None),
            P("section", "tensor"),
        ),
        out_specs=(
            P("section", "tensor", None, None, None),
            P("section", "tensor", None, None, None),
            P("section", "tensor"),
            P("section", "tensor", None),
        ),
        check_vma=False,
    )
```

profile of v0, /device:TPU:0, one launch (start us, length us, event | category | flops | bytes accessed | tf_op | source)
XLA Modules:
  0.0 327.6 jit_solution(7803995494779378188)
XLA Ops:
  7.2 0.0 all-gather.3.cloned.1.call-start
  7.2 0.7 all-gather.3.cloned.1.call-update
  7.9 0.0 all-gather.5.cloned.1.call-start
  7.9 0.7 all-gather.5.cloned.1.call-update
  8.6 0.0 reduce-scatter.5.cloned.1.call-start
  8.7 0.7 broadcast_compare_fusion.1
  9.4 0.1 copy.58
  9.5 0.8 copy.45
  10.3 0.7 compare_select_fusion.1
  10.9 0.1 copy.38
  11.0 0.1 reshape.122
  11.1 0.7 compare_select_fusion
  11.8 0.1 copy.40
  11.9 0.1 reshape.130
  12.0 0.7 broadcast_compare_fusion
  12.7 0.1 copy.59
  12.8 0.1 reshape_squeeze.15
  12.9 10.8 %all_gather.11 = bf16[1,32768]{1,0:T(2,128)(2,1)S(1)} all-gather(bf16[1,4096]{1,0:T(2,128)(2,1)} %param.14), channel_id=1, replica_groups=mesh['section'=4,'tensor'=8] {'tensor'}, dimensions={1}, use_global_device_ids=true | all-gather | bytes 73728 | tf_op jit(solution)/shard_map/all_gather | solution.py:31
  23.8 0.4 reduce
  24.2 0.8 fusion.21
  25.0 15.6 %all-gather.3.cloned.1.call-done = bf16[1,8192,128]{2,1,0:T(8,128)(2,1)} async-done(((bf16[1,1024,128]{2,1,0:T(8,128)(2,1)}), bf16[1,8192,128]{2,1,0:T(8,128)(2,1)}) %all-gather.3.cloned.1.call-update) | async-done | bytes 2097168 | tf_op jit(solution)/shard_map/all_gather | solution.py:29
  40.7 9.7 %gather_fusion = bf16[192,128,128]{2,1,0:T(8,128)(2,1)} fusion(bf16[64,128,128]{2,1,0:T(8,128)(2,1)} %bitcast.84, s32[1024]{0:T(1024)S(1)} %pad_clamp_fusion.1), kind=kCustom, calls=%fused_computation | custom fusion | bytes 12583680 | tf_op jit(solution)/shard_map/gather | solution.py:48
  50.4 20.1 %all-gather.5.cloned.1.call-done = bf16[1,8192,128]{2,1,0:T(8,128)(2,1)} async-done(((bf16[1,1024,128]{2,1,0:T(8,128)(2,1)}), bf16[1,8192,128]{2,1,0:T(8,128)(2,1)}) %all-gather.5.cloned.1.call-update) | async-done | bytes 2097168 | tf_op jit(solution)/shard_map/all_gather | solution.py:30
  70.5 9.7 %gather_fusion.1 = bf16[192,128,128]{2,1,0:T(8,128)(2,1)} fusion(bf16[64,128,128]{2,1,0:T(8,128)(2,1)} %bitcast.85, s32[1024]{0:T(1024)S(1)} %pad_clamp_fusion), kind=kCustom, calls=%fused_computation.1 | custom fusion | bytes 12583680 | tf_op jit(solution)/shard_map/gather | solution.py:49
  80.2 8.2 %fusion.5 = f32[32,128,128,1]{1,2,3,0:T(8,128)} fusion(bf16[32,6,128,128]{3,2,1,0:T(8,128)(2,1)} %bitcast.86, bf16[1,32,6,128,128]{4,3,2,1,0:T(8,128)(2,1)} %param.12, pred[32,6]{1,0:T(8,128)(4,1)S(1)} %bitcast.92), kind=kOutput, calls=%fused_computation.12 | convolution fusion | flops 808452096 | bytes 14680256 | tf_op jit(solution)/shard_map/rsij,rsjt->rit/dot_general | solution.py:51
  88.4 0.0 copy-done
  88.4 6.0 %fusion.29 = (f32[32,128]{1,0:T(8,128)S(1)}, bf16[32,128,128]{1,2,0:T(8,128)(2,1)}) fusion(f32[32,128]{1,0:T(8,128)S(1)} %fusion.21, f32[32,128,128,1]{1,2,3,0:T(8,128)} %fusion.5, bf16[32,6,128,128]{3,2,1,0:T(8,128)(2,1)S(1)} %bitcast.89, bf16[1,32,6,128,128]{4,3,2,1,0:T(8,128)(2,1)} %param.13, pred[32,6]{1,0:T(8,128)(4,1)S(1)} %bitcast.96), kind=kOutput, calls=%fused_computation.47 | convolution fusion | flops 814739456 | bytes 15761600 | tf_op jit(solution)/shard_map/rsij,rsjt->rit/dot_general | solution.py:56
  94.4 9.7 %fusion.4 = f32[32,6,128,128]{3,2,1,0:T(8,128)} fusion(bf16[1,32,6,128,128]{4,3,2,1,0:T(8,128)(2,1)} %param.12, pred[32,6]{1,0:T(8,128)(4,1)S(1)} %bitcast.93, bf16[32,128,128]{1,2,0:T(8,128)(2,1)} %get-tuple-element.17), kind=kOutput, calls=%fused_computation.11 | convolution fusion | flops 808452096 | bytes 19923136 | tf_op jit(solution)/shard_map/rsij,rit->rsjt/dot_general | solution.py:65
  104.1 2.5 broadcast_in_dim.50
  106.6 39.5 %scatter_fusion = f32[64,128,128]{2,1,0:T(8,128)} fusion(f32[64,128,128]{2,1,0:T(8,128)} %broadcast_in_dim.50, s32[192]{0:T(256)S(1)} %bitcast.95, f32[192,128,128]{2,1,0:T(8,128)} %bitcast.83), kind=kCustom, calls=%fused_computation.2 | custom fusion | flops 3145728 | bytes 37749504 | tf_op jit(solution)/shard_map/scatter-add | solution.py:66
  146.1 0.0 reduce-scatter.5.cloned.1.call-update
  146.1 0.0 reduce-scatter.7.cloned.1.call-start
  146.2 0.0 copy-done.2
  146.2 0.4 fusion.23
  146.6 8.4 %copy.66 = f32[1,32768]{0,1:T(8,128)} copy(f32[1,32768]{1,0:T(1,128)S(1)} %bitcast.91) | data formatting | bytes 262144
  155.0 6.1 %fusion.1 = bf16[1,32,6,128,128]{3,4,2,1,0:T(8,128)(2,1)} fusion(pred[32,6]{1,0:T(8,128)(4,1)S(1)} %bitcast.97, bf16[32,6,128,128]{3,2,1,0:T(8,128)(2,1)} %bitcast.88, f32[32,128,128,1]{1,2,3,0:T(8,128)S(1)} %copy-done.3, f32[32,128]{1,0:T(8,128)S(1)} %fusion.21), kind=kOutput, calls=%fused_computation.6 | convolution fusion | flops 814743552 | bytes 14696640 | tf_op jit(solution)/shard_map/rit,rsjt->rsij/dot_general | solution.py:61
  161.1 0.0 reduce-scatter.7.cloned.1.call-update
  161.1 36.6 %reduce-scatter.5.cloned.1.call-done = f32[1,1024,128]{2,1,0:T(8,128)} async-done(((f32[1,8192,128]{2,1,0:T(8,128)}), f32[1,1024,128]{2,1,0:T(8,128)}) %reduce-scatter.5.cloned.1.call-update) | async-done | bytes 524304 | tf_op jit(solution)/shard_map/reduce_scatter | solution.py:74
  197.7 1.1 convert_element_type.29
  198.8 3.4 %collective-permute-start = (bf16[1,1024,128]{2,1,0:T(8,128)(2,1)S(1)}, bf16[1,1024,128]{2,1,0:T(8,128)(2,1)S(1)}, u32[]{:S(2)}, u32[]{:S(2)}) collective-permute-start(bf16[1,1024,128]{2,1,0:T(8,128)(2,1)S(1)} %convert_element_type.29), channel_id=1, source_target_pairs={{0,24},{8,0},{16,8},{24,16},{1,25},{9,1},{17,9},{25,17},{2,26},{10... | collective-permute-start | bytes 786440 | tf_op jit(solution)/shard_map/ppermute | solution.py:16
  202.2 0.0 copy-done.1
  202.2 7.2 %fusion = bf16[1,32,6,128,128]{3,4,2,1,0:T(8,128)(2,1)} fusion(pred[32,6]{1,0:T(8,128)(4,1)S(1)} %bitcast.94, bf16[32,6,128,128]{3,2,1,0:T(8,128)(2,1)} %bitcast.87, bf16[32,128,128]{1,2,0:T(8,128)(2,1)S(1)} %copy-done.1), kind=kOutput, calls=%fused_computation.5 | convolution fusion | flops 811597824 | bytes 13631680 | tf_op jit(solution)/shard_map/rit,rsjt->rsij/dot_general | solution.py:63
  209.4 9.3 %copy.48 = bf16[1,32,6,128,128]{4,3,2,1,0:T(8,128)(2,1)} copy(bf16[1,32,6,128,128]{3,4,2,1,0:T(8,128)(2,1)} %fusion) | data formatting | bytes 12582912
  218.7 9.2 %copy.49 = bf16[1,32,6,128,128]{4,3,2,1,0:T(8,128)(2,1)} copy(bf16[1,32,6,128,128]{3,4,2,1,0:T(8,128)(2,1)} %fusion.1) | data formatting | bytes 12582912
  227.9 89.7 %reduce-scatter.7.cloned.1.call-done = f32[4096,1]{1,0:T(8,128)} async-done(((f32[32768,1]{1,0:T(8,128)}), f32[4096,1]{1,0:T(8,128)}) %reduce-scatter.7.cloned.1.call-update) | async-done | bytes 16400
  317.5 2.8 copy.67
  320.3 0.0 collective-permute-done
  320.3 0.7 copy.70
  (8 shorter events, 0.0 us)
Async XLA Ops:
  7.2 33.5 %all-gather.3.cloned.1.call-start = ((), (), s32[]{:S(2)}) async-start(), calls=%async_computation.2 | async-start | bytes 2359296 | tf_op jit(solution)/shard_map/all_gather | solution.py:29
  7.9 62.6 %all-gather.5.cloned.1.call-start = ((), (), s32[]{:S(2)}) async-start(), calls=%async_computation.3 | async-start | bytes 2359296 | tf_op jit(solution)/shard_map/all_gather | solution.py:30
  8.6 189.1 %reduce-scatter.5.cloned.1.call-start = ((), (), s32[]{:S(2)}) async-start(), calls=%async_computation.4 | async-start | bytes 4718592 | tf_op jit(solution)/shard_map/reduce_scatter | solution.py:74
  80.2 8.2 %copy-start = (bf16[192,128,128]{2,1,0:T(8,128)(2,1)S(1)}, bf16[192,128,128]{2,1,0:T(8,128)(2,1)}, u32[]{:S(2)}) copy-start(bf16[192,128,128]{2,1,0:T(8,128)(2,1)} %gather_fusion.1) | copy-start | bytes 18874372
  106.6 39.6 %copy-start.2 = (s32[1,32]{1,0:T(1,128)S(1)}, s32[1,32]{1,0:T(1,128)}, u32[]{:S(2)}) copy-start(s32[1,32]{1,0:T(1,128)} %param.19) | copy-start | bytes 388
  146.1 171.4 %reduce-scatter.7.cloned.1.call-start = ((), (), s32[]{:S(2)}) async-start(), calls=%async_computation.5 | async-start | bytes 18874368
  146.6 8.4 %copy-start.3 = (f32[32,128,128,1]{1,2,3,0:T(8,128)S(1)}, f32[32,128,128,1]{1,2,3,0:T(8,128)}, u32[]{:S(2)}) copy-start(f32[32,128,128,1]{1,2,3,0:T(8,128)} %fusion.5) | copy-start | bytes 6291460
  161.1 41.1 %copy-start.1 = (bf16[32,128,128]{1,2,0:T(8,128)(2,1)S(1)}, bf16[32,128,128]{1,2,0:T(8,128)(2,1)}, u32[]{:S(2)}) copy-start(bf16[32,128,128]{1,2,0:T(8,128)(2,1)} %get-tuple-element.17) | copy-start | bytes 3145732
  198.8 121.5 %collective-permute-start = (bf16[1,1024,128]{2,1,0:T(8,128)(2,1)S(1)}, bf16[1,1024,128]{2,1,0:T(8,128)(2,1)S(1)}, u32[]{:S(2)}, u32[]{:S(2)}) collective-permute-start(bf16[1,1024,128]{2,1,0:T(8,128)(2,1)S(1)} %convert_element_type.29), channel_id=1, source_target_pairs={{0,24},{8,0},{16,8},{24,16},{1,25},{9,1},{17,9},{25,17},{2,26},{10... | collective-permute-start | bytes 786440 | tf_op jit(solution)/shard_map/ppermute | solution.py:16
Sparse Core Ops, SparseCore 0:
  9.9 30.7 all-gather.2
  42.6 27.8 all-gather.4
  146.3 51.4 reduce-scatter.4
  201.6 115.9 reduce-scatter.6
where the time goes:
time: 329 us; the launch traced here: 328 us
  waiting for transfers between devices  163 us (50%)
  local copies, waits for them, and re-layouts  53.8 us (16%)
  other arithmetic  43.7 us (13%)
  matrix products  38.4 us (12%)
  between operations  13.8 us (4%)
  blocking collectives  10.8 us (3%)
  starting transfers between devices  3.54 us (1%)
    unnamed x5, waiting for transfers between devices  91.1 us
    scatter-add x1, other arithmetic, local(): zero_grad.at[col_in.reshape(-1)].add(pieces.reshape(-1, BLK, TOK))  39.5 us
    reduce_scatter x1, waiting for transfers between devices, local(): lax.psum_scatter(input_terms, 'tensor', scatter_dimension=1, tiled=True)  36.6 us
    unnamed x14, local copies, waits for them, and re-layouts  31.2 us
    all_gather x1, waiting for transfers between devices, local(): lax.all_gather(out_grads, 'tensor', axis=1, tiled=True)  20.1 us
    all_gather x1, waiting for transfers between devices, local(): lax.all_gather(activations, 'tensor', axis=1, tiled=True)  15.6 us
    all_gather x1, blocking collectives, local(): lax.all_gather(bias_in, 'tensor', axis=1, tiled=True)  10.8 us
    dot_general x1, matrix products, local(): jnp.einsum('rsij,rit->rsjt', w_keep_in, grad_low, preferred_element_type=...  9.68 us
  transfers between devices with their start and end apart: 5, of which 4 were waited for; matrix products, arithmetic and copies ran while one was open for 18% of the time, Pallas kernels for 0%

commit v1 on v0

v1 whole, which is shorter than its diff:
```python
import functools

import jax
import jax.numpy as jnp
from jax import lax
from jax.experimental import pallas as pl
from jax.experimental.pallas import tpu as pltpu
from jax.sharding import PartitionSpec as P

BLK = 128
MESH = pl.DeviceIdType.MESH
BF16 = jnp.bfloat16
F32 = jnp.float32


def gelu_parts(pre_act):
    cdf_part = 0.5 * (1.0 + lax.erf(pre_act * 0.7071067811865476))
    density = jnp.exp(-0.5 * pre_act * pre_act) * 0.3989422804014327
    return (pre_act * cdf_part, cdf_part + pre_act * density)


def gather_kernel(
    tensor, act, grad, bias, act_all, grad_all, bias_all, send, recv, fsend, frecv, own
):
    chips = tensor // 2
    me = lax.axis_index("tensor")
    sec = lax.axis_index("section")
    core = lax.rem(me, 2)
    chip = me // 2
    partner = chip * 2 + (1 - core)
    sources = (act, grad, bias)
    results = (act_all, grad_all, bias_all)

    def other(step):
        return lax.rem(chip + step, chips) * 2 + core

    def behind(step):
        return lax.rem(chip + chips - step, chips) * 2 + core

    barrier = pltpu.get_barrier_semaphore()
    for peer in [partner] + [other(step) for step in range(1, chips)]:
        pl.semaphore_signal(barrier, inc=1, device_id=(sec, peer), device_id_type=MESH)
    pl.semaphore_wait(barrier, chips)

    def far(kind, step):
        return pltpu.make_async_remote_copy(
            src_ref=sources[kind],
            dst_ref=results[kind].at[me],
            send_sem=send.at[kind, step],
            recv_sem=recv.at[kind, step],
            device_id=(sec, other(step)),
            device_id_type=MESH,
        )

    def near(kind, step):
        slot = behind(step)
        return pltpu.make_async_remote_copy(
            src_ref=sources[kind] if step == 0 else results[kind].at[slot],
            dst_ref=results[kind].at[slot],
            send_sem=fsend.at[kind, step],
            recv_sem=frecv.at[kind, step],
            device_id=(sec, partner),
            device_id_type=MESH,
        )

    order = (2, 0, 1)
    for kind in order:
        for step in range(1, chips):
            far(kind, step).start()
    for kind in order:
        near(kind, 0).start()
        pltpu.make_async_copy(sources[kind], results[kind].at[me], own.at[kind]).start()
    for kind in order:
        for step in range(1, chips):
            far(kind, step).wait_recv()
            near(kind, step).start()
    for kind in order:
        pltpu.make_async_copy(sources[kind], results[kind].at[me], own.at[kind]).wait()
        for step in range(1, chips):
            far(kind, step).wait_send()
        for step in range(chips):
            near(kind, step).wait()


def row_kernel(
    slots, rows, dblocks, tensor,
    cols_in, mask_in, cols_out, mask_out, stored,
    w_in, w_out, act, grad, bias,
    hidden_out, low_out, part_out, bias_out,
    total, bias_wide,
):
    row = pl.program_id(0)
    hblocks = rows * tensor

    @pl.when(row == 0)
    def _():
        total[...] = jnp.zeros_like(total)
        bias_out[...] = jnp.zeros_like(bias_out)
        bias_wide[...] = bias[...].reshape(hblocks, BLK).astype(F32)

    def wide(ref):
        return jnp.concatenate([ref[0, s] for s in range(slots)], axis=1)

    def tall(ref, cols, mask):
        return jnp.concatenate(
            [
                jnp.where(mask[row, s] > 0, ref[cols[row, s]], jnp.zeros((BLK, BLK), BF16))
                for s in range(slots)
            ],
            axis=0,
        )

    w_wide = wide(w_in)
    where_row = stored[row]
    bias_row = bias_wide[pl.ds(where_row, 1), :]
    bias_col = jnp.transpose(jnp.broadcast_to(bias_row, (BLK, BLK)))
    pre_act = jnp.dot(w_wide, tall(act, cols_in, mask_in), preferred_element_type=F32) + bias_col
    act_value, slope = gelu_parts(pre_act)
    hidden_out[0] = act_value.astype(BF16)
    grad_hidden = jnp.dot(
        wide(w_out), tall(grad, cols_out, mask_out), preferred_element_type=F32
    )
    grad_pre = grad_hidden * slope
    low_out[0] = grad_pre.astype(BF16)
    turned = jnp.transpose(grad_pre)
    bias_out[pl.ds(where_row, 1), :] = jnp.sum(turned, axis=0, keepdims=True)
    pieces = jnp.dot(turned.astype(BF16), w_wide, preferred_element_type=F32)
    for s in range(slots):

        @pl.when(mask_in[row, s] > 0)
        def _():
            total[cols_in[row, s]] += pieces[:, s * BLK : (s + 1) * BLK]

    @pl.when(row == rows - 1)
    def _():
        chips = tensor // 2
        per = dblocks // tensor
        for chip in range(chips):
            for core in range(2):
                base = (chip * 2 + core) * per
                part_out[core, chip] = total[base : base + per].astype(BF16)


def scatter_kernel(
    tensor, sections, slots, rows, per,
    cols_in, mask_in, cols_out, mask_out,
    part, bias_part, hidden, low, act, grad,
    tiles_in, tiles_out, bias_sum, handed,
    held_in, held_out, from_pair, pair_sum, from_chips, final, bias_from, bias_keep,
    pair_send, pair_recv, chip_send, chip_recv, bias_send, bias_recv, hand_send, hand_recv, store,
):
    chips = tensor // 2
    me = lax.axis_index("tensor")
    sec = lax.axis_index("section")
    core = lax.rem(me, 2)
    chip = me // 2
    partner = chip * 2 + (1 - core)
    before = lax.rem(sec + sections - 1, sections)
    after = lax.rem(sec + 1, sections)

    def ahead_chip(step):
        return lax.rem(chip + step, chips)

    barrier = pltpu.get_barrier_semaphore()
    for step in range(1, tensor):
        pl.semaphore_signal(
            barrier, inc=1, device_id=(sec, lax.rem(me + step, tensor)), device_id_type=MESH
        )
    for section in (before, after):
        pl.semaphore_signal(barrier, inc=1, device_id=(section, me), device_id_type=MESH)
    pl.semaphore_wait(barrier, tensor + 1)

    pair = pltpu.make_async_remote_copy(
        src_ref=part.at[1 - core],
        dst_ref=from_pair,
        send_sem=pair_send,
        recv_sem=pair_recv,
        device_id=(sec, partner),
        device_id_type=MESH,
    )
    pair.start()

    def bias_copy(step):
        peer = lax.rem(me + step, tensor)
        return pltpu.make_async_remote_copy(
            src_ref=bias_part.at[peer],
            dst_ref=bias_from.at[step],
            send_sem=bias_send.at[step],
            recv_sem=bias_recv.at[step],
            device_id=(sec, peer),
            device_id_type=MESH,
        )

    for step in range(1, tensor):
        bias_copy(step).start()

    def chip_copy(step):
        return pltpu.make_async_remote_copy(
            src_ref=pair_sum.at[step],
            dst_ref=from_chips.at[step],
            send_sem=chip_send.at[step],
            recv_sem=chip_recv.at[step],
            device_id=(sec, ahead_chip(step) * 2 + core),
            device_id_type=MESH,
        )

    def tall(ref, cols, mask, row):
        return jnp.concatenate(
            [
                jnp.where(mask[row, s] > 0, ref[cols[row, s]], jnp.zeros((BLK, BLK), BF16))
                for s in range(slots)
            ],
            axis=0,
        )

    def out_product(left, right):
        return lax.dot_general(
            left, right, (((1,), (1,)), ((), ())), preferred_element_type=F32
        ).astype(BF16)

    def one_row(row, carry):
        got_in = out_product(low[row], tall(act, cols_in, mask_in, row))
        got_out = out_product(hidden[row], tall(grad, cols_out, mask_out, row))
        for s in range(slots):
            held_in[row, s] = got_in[:, s * BLK : (s + 1) * BLK]
            held_out[row, s] = got_out[:, s * BLK : (s + 1) * BLK]
        pltpu.make_async_copy(held_in.at[row], tiles_in.at[row], store.at[0]).start()
        pltpu.make_async_copy(held_out.at[row], tiles_out.at[row], store.at[1]).start()
        return carry

    first, second = rows // 4, rows - rows // 4
    lax.fori_loop(0, first, one_row, 0)

    pair.wait()
    for step in list(range(1, chips)) + [0]:
        where_chip = ahead_chip(step)
        pair_sum[step] = (
            part[core, where_chip].astype(F32) + from_pair[where_chip].astype(F32)
        ).astype(BF16)
        if step:
            chip_copy(step).start()

    lax.fori_loop(first, second, one_row, 0)

    result = pair_sum[0].astype(F32)
    for step in range(1, chips):
        chip_copy(step).wait()
        result = result + from_chips[step].astype(F32)
    for block in range(per):
        final[block] = jnp.transpose(result[block]).astype(BF16)
    hand = pltpu.make_async_remote_copy(
        src_ref=final,
        dst_ref=handed,
        send_sem=hand_send,
        recv_sem=hand_recv,
        device_id=(before, me),
        device_id_type=MESH,
    )
    hand.start()

    lax.fori_loop(second, rows, one_row, 0)

    bias_total = bias_part[me]
    for step in range(1, tensor):
        bias_copy(step).wait()
        bias_total = bias_total + bias_from[step]
    bias_keep[...] = bias_total
    keep = pltpu.make_async_copy(bias_keep, bias_sum, store.at[2])
    keep.start()
    keep.wait()
    hand.wait()
    pltpu.make_async_copy(held_in, tiles_in, store.at[0]).wait()
    pltpu.make_async_copy(held_out, tiles_out, store.at[1]).wait()


def local(
    activations, out_grads, w_in, w_out, bias_in, cols_in, mask_in, cols_out, mask_out, block_rows
):
    tensor = lax.axis_size("tensor")
    sections = lax.axis_size("section")
    chips = tensor // 2
    _, rows, slots = cols_in.shape
    depth = activations.shape[1]
    per = depth // BLK
    dblocks = per * tensor
    hblocks = rows * tensor
    any_spec = pl.BlockSpec(memory_space=pl.ANY)
    vmem_spec = pl.BlockSpec(memory_space=pltpu.VMEM)
    smem_spec = pl.BlockSpec(memory_space=pltpu.SMEM)
    dma = pltpu.SemaphoreType.DMA

    act_all, grad_all, bias_all = pl.pallas_call(
        functools.partial(gather_kernel, tensor),
        out_shape=(
            jax.ShapeDtypeStruct((tensor, per, BLK, BLK), BF16),
            jax.ShapeDtypeStruct((tensor, per, BLK, BLK), BF16),
            jax.ShapeDtypeStruct((tensor, rows, BLK), BF16),
        ),
        in_specs=[any_spec] * 3,
        out_specs=[any_spec] * 3,
        scratch_shapes=[dma((3, chips))] * 4 + [dma((3,))],
        compiler_params=pltpu.CompilerParams(collective_id=0, has_side_effects=True),
        name="gather_inputs",
    )(
        activations.reshape(per, BLK, BLK),
        out_grads.reshape(per, BLK, BLK),
        bias_in.reshape(rows, BLK),
    )
    act_all = act_all.reshape(dblocks, BLK, BLK)
    grad_all = grad_all.reshape(dblocks, BLK, BLK)

    def whole(*shape):
        return pl.BlockSpec(shape, lambda row, *_: (0,) * len(shape))

    tile_spec = pl.BlockSpec((1, slots, BLK, BLK), lambda row, *_: (row, 0, 0, 0))
    block_spec = pl.BlockSpec((1, BLK, BLK), lambda row, *_: (row, 0, 0))
    hidden, low, part, bias_part = pl.pallas_call(
        functools.partial(row_kernel, slots, rows, dblocks, tensor),
        out_shape=(
            jax.ShapeDtypeStruct((rows, BLK, BLK), BF16),
            jax.ShapeDtypeStruct((rows, BLK, BLK), BF16),
            jax.ShapeDtypeStruct((2, chips, per, BLK, BLK), BF16),
            jax.ShapeDtypeStruct((hblocks, BLK), F32),
        ),
        grid_spec=pltpu.PrefetchScalarGridSpec(
            num_scalar_prefetch=5,
            grid=(rows,),
            in_specs=[
                tile_spec,
                tile_spec,
                whole(dblocks, BLK, BLK),
                whole(dblocks, BLK, BLK),
                whole(tensor, rows, BLK),
            ],
            out_specs=[
                block_spec,
                block_spec,
                whole(2, chips, per, BLK, BLK),
                whole(hblocks, BLK),
            ],
            scratch_shapes=[
                pltpu.VMEM((dblocks, BLK, BLK), F32),
                pltpu.VMEM((hblocks, BLK), F32),
            ],
        ),
        compiler_params=pltpu.CompilerParams(vmem_limit_bytes=48 << 20),
        name="rows",
    )(
        cols_in[0], mask_in[0], cols_out[0], mask_out[0], block_rows[0],
        w_in[0], w_out[0], act_all, grad_all, bias_all,
    )

    tiles_in, tiles_out, bias_sum, handed = pl.pallas_call(
        functools.partial(scatter_kernel, tensor, sections, slots, rows, per),
        out_shape=(
            jax.ShapeDtypeStruct((rows, slots, BLK, BLK), BF16),
            jax.ShapeDtypeStruct((rows, slots, BLK, BLK), BF16),
            jax.ShapeDtypeStruct((rows, BLK), F32),
            jax.ShapeDtypeStruct((per, BLK, BLK), BF16),
        ),
        in_specs=[smem_spec] * 4 + [vmem_spec] * 6,
        out_specs=[any_spec] * 4,
        scratch_shapes=[
            pltpu.VMEM((rows, slots, BLK, BLK), BF16),
            pltpu.VMEM((rows, slots, BLK, BLK), BF16),
            pltpu.VMEM((chips, per, BLK, BLK), BF16),
            pltpu.VMEM((chips, per, BLK, BLK), BF16),
            pltpu.VMEM((chips, per, BLK, BLK), BF16),
            pltpu.VMEM((per, BLK, BLK), BF16),
            pltpu.VMEM((tensor, rows, BLK), F32),
            pltpu.VMEM((rows, BLK), F32),
            dma(()), dma(()),
            dma((chips,)), dma((chips,)),
            dma((tensor,)), dma((tensor,)),
            dma(()), dma(()),
            dma((3,)),
        ],
        compiler_params=pltpu.CompilerParams(
            collective_id=1, has_side_effects=True, vmem_limit_bytes=48 << 20
        ),
        name="scatter_tiles",
    )(
        cols_in[0], mask_in[0], cols_out[0], mask_out[0],
        part, bias_part.reshape(tensor, rows, BLK), hidden, low, act_all, grad_all,
    )
    return (
        tiles_in[None],
        tiles_out[None],
        bias_sum.reshape(1, rows * BLK),
        handed.reshape(1, depth, BLK),
    )


def solution(mesh):
    return jax.shard_map(
        local,
        mesh=mesh,
        in_specs=(
            P("section", "tensor", None),
            P("section", "tensor", None),
            P("section", "tensor", None, None, None),
            P("section", "tensor", None, None, None),
            P("section", "tensor"),
            P("section", "tensor", None),
            P("section", "tensor", None),
            P("section", "tensor", None),
            P("section", "tensor", None),
            P("section", "tensor"),
        ),
        out_specs=(
            P("section", "tensor", None, None, None),
            P("section", "tensor", None, None, None),
            P("section", "tensor"),
            P("section", "tensor", None),
        ),
        check_vma=False,
    )
```

time: 329 us -> 109 us (0.33)
  waiting for transfers between devices: 163 us -> 0 us
  Pallas kernels: 0 us -> 89.6 us
  other arithmetic: 43.7 us -> 1.37 us
  matrix products: 38.4 us -> 0 us
  local copies, waits for them, and re-layouts: 53.8 us -> 16.8 us
  between operations: 13.8 us -> 0.68 us
  blocking collectives: 10.8 us -> 0 us
  starting transfers between devices: 3.54 us -> 0 us
    unnamed x5 -> x0, waiting for transfers between devices: 91.1 us -> none
    pallas_call x0 -> x3, Pallas kernels: none -> 89.6 us  [the longest x1 30.7 us: local(): pl.pallas_call(functools.partial(row_kernel, slots, rows, dblocks, tensor...]
    scatter-add x1 -> x0, other arithmetic: 39.5 us -> none  [local(): zero_grad.at[col_in.reshape(-1)].add(pieces.reshape(-1, BLK, TOK))]
    dot_general x7 -> x0, matrix products: 38.4 us -> none  [the longest x1 9.68 us: local(): jnp.einsum('rsij,rit->rsjt', w_keep_in, grad_low, preferred_element_type=...]
    reduce_scatter x1 -> x0, waiting for transfers between devices: 36.6 us -> none  [local(): lax.psum_scatter(input_terms, 'tensor', scatter_dimension=1, tiled=True)]
    all_gather x2 -> x0, waiting for transfers between devices: 35.8 us -> none  [the longest x1 20.1 us: local(): lax.all_gather(out_grads, 'tensor', axis=1, tiled=True)]
    gather x2 -> x0, local copies, waits for them, and re-layouts: 19.4 us -> none  [the longest x1 9.68 us: local(): slots_grad = grad_blocks[col_out]]
    unnamed x14, local copies, waits for them, and re-layouts: 31.2 us -> 16.8 us
  transfers between devices with their start and end apart: 5 -> 0, of which waited for: 4 -> 0; matrix products, arithmetic and copies ran while one was open for 18% -> 0% of each run, Pallas kernels for 0% -> 0%
where the time goes in v1:
time: 109 us; the launch traced here: 108 us
  Pallas kernels  89.6 us (82%)
  local copies, waits for them, and re-layouts  16.8 us (15%)
  other arithmetic  1.37 us (1%)
    pallas_call x1, Pallas kernels, local(): pl.pallas_call(functools.partial(row_kernel, slots, rows, dblocks, tensor...  30.7 us
    pallas_call x1, Pallas kernels, local(): pl.pallas_call(functools.partial(gather_kernel, tensor), out_shape=(jax.S...  30.4 us
    pallas_call x1, Pallas kernels, local(): pl.pallas_call(functools.partial(scatter_kernel, tensor, sections, slots,...  28.5 us
    unnamed x14, local copies, waits for them, and re-layouts  16.8 us

profile of v1, /device:TPU:0, one launch (start us, length us, event | category | flops | bytes accessed | tf_op | source)
XLA Modules:
  0.0 108.5 jit_solution(15881510615987214350)
XLA Ops:
  0.6 1.4 %reduce = bf16[4096]{0:T(1024)(128)(2,1)} reduce(bf16[1,4096]{1,0:T(2,128)(2,1)} %param.14, bf16[]{:T(256)} %constant.10), dimensions={0}, to_apply=%param.14.reduce_sub_computation | reduce | bytes 16386 | tf_op args[4]
  2.0 0.8 copy.14
  2.8 0.8 copy.15
  3.5 0.8 copy.16
  4.3 0.8 copy.17
  5.1 30.4 %gather_inputs.1 = (bf16[8,8,128,128]{3,2,1,0:T(8,128)(2,1)}, bf16[8,8,128,128]{3,2,1,0:T(8,128)(2,1)}, bf16[8,32,128]{2,1,0:T(8,128)(2,1)}) custom-call(bf16[8,128,128]{2,1,0:T(8,128)(2,1)} %bitcast.37, bf16[8,128,128]{2,1,0:T(8,128)(2,1)} %bitcast.38, bf16[32,128]{1,0:T(8,128)(2,1)} %bitcast.39), custom_call_target="tpu_custom_call" | custom-call | tf_op jit(solution)/shard_map/gather_inputs/pallas_call | solution.py:292
  35.4 0.0 copy-start
  35.4 0.8 copy-done
  36.3 0.0 copy-start.1
  36.3 0.7 copy-done.1
  36.9 30.7 %rows.1 = (bf16[32,128,128]{2,1,0:T(8,128)(2,1)S(1)}, bf16[32,128,128]{2,1,0:T(8,128)(2,1)S(1)}, bf16[2,4,8,128,128]{4,3,2,1,0:T(8,128)(2,1)S(1)}, f32[256,128]{1,0:T(8,128)S(1)}) custom-call(s32[32,6]{1,0:T(8,128)S(1)} %bitcast.18, s32[32,6]{1,0:T(8,128)S(1)} %bitcast.20, s32[32,6]{1,0:T(8,128)S(1)} %bitcast.22, s32[32,6]{1,0:T(8,128)S(1)} %bitcast.24, ...), custom_call_target="tpu_custom_call" | custom-call | tf_op jit(solution)/shard_map/rows/pallas_call | solution.py:317
  67.6 28.5 %scatter_tiles.1 = (bf16[32,6,128,128]{3,2,1,0:T(8,128)(2,1)}, bf16[32,6,128,128]{3,2,1,0:T(8,128)(2,1)}, f32[32,128]{1,0:T(8,128)S(1)}, bf16[8,128,128]{2,1,0:T(8,128)(2,1)S(1)}) custom-call(s32[32,6]{1,0:T(8,128)S(1)} %bitcast.19, s32[32,6]{1,0:T(8,128)S(1)} %bitcast.21, s32[32,6]{1,0:T(8,128)S(1)} %bitcast.23, s32[32,6]{1,0:T(8,128)S(1)} %bitcast.25, ...), custom_call_target="tpu_custom_call" | custom-call | tf_op jit(solution)/shard_map/scatter_tiles/pallas_call | solution.py:353
  96.2 0.0 copy-start.2
  96.2 8.3 %copy.22 = bf16[1,32,6,128,128]{4,3,2,1,0:T(8,128)(2,1)} copy(bf16[1,32,6,128,128]{4,3,2,1,0:T(8,128)(2,1)} %bitcast.36) | data formatting | bytes 12582912
  104.5 0.0 copy-done.2
  104.5 2.7 %copy.23 = bf16[1,32,6,128,128]{4,3,2,1,0:T(8,128)(2,1)} copy(bf16[1,32,6,128,128]{4,3,2,1,0:T(8,128)(2,1)S(1)} %bitcast.35) | data formatting | bytes 12582912
  107.2 0.6 copy.24
  107.8 0.7 copy.25
Async XLA Ops:
  35.4 0.8 copy-start
  36.3 0.7 copy-start.1
  96.2 8.3 %copy-start.2 = (bf16[32,6,128,128]{3,2,1,0:T(8,128)(2,1)S(1)}, bf16[32,6,128,128]{3,2,1,0:T(8,128)(2,1)}, u32[]{:S(2)}) copy-start(bf16[32,6,128,128]{3,2,1,0:T(8,128)(2,1)} %get-tuple-element.23) | copy-start | bytes 18874372

commit v2 on v1

--- a/solution.py
+++ b/solution.py
@@ -82,56 +82,75 @@
             near(kind, step).wait()
 
 
+def tall(ref, meta, row, slots, first):
+    return jnp.concatenate(
+        [
+            jnp.where(
+                meta[first + slots + s, row] > 0,
+                ref[meta[first + s, row]],
+                jnp.zeros((BLK, BLK), BF16),
+            )
+            for s in range(slots)
+        ],
+        axis=0,
+    )
+
+
 def row_kernel(
-    slots, rows, dblocks, tensor,
-    cols_in, mask_in, cols_out, mask_out, stored,
+    slots, group, dblocks, tensor,
+    meta, stored,
     w_in, w_out, act, grad, bias,
     hidden_out, low_out, part_out, bias_out,
     total, bias_wide,
 ):
-    row = pl.program_id(0)
-    hblocks = rows * tensor
-
-    @pl.when(row == 0)
+    step = pl.program_id(0)
+    hblocks = bias_wide.shape[0]
+
+    @pl.when(step == 0)
     def _():
         total[...] = jnp.zeros_like(total)
         bias_out[...] = jnp.zeros_like(bias_out)
         bias_wide[...] = bias[...].reshape(hblocks, BLK).astype(F32)
 
-    def wide(ref):
-        return jnp.concatenate([ref[0, s] for s in range(slots)], axis=1)
-
-    def tall(ref, cols, mask):
-        return jnp.concatenate(
-            [
-                jnp.where(mask[row, s] > 0, ref[cols[row, s]], jnp.zeros((BLK, BLK), BF16))
-                for s in range(slots)
-            ],
-            axis=0,
-        )
-
-    w_wide = wide(w_in)
-    where_row = stored[row]
-    bias_row = bias_wide[pl.ds(where_row, 1), :]
-    bias_col = jnp.transpose(jnp.broadcast_to(bias_row, (BLK, BLK)))
-    pre_act = jnp.dot(w_wide, tall(act, cols_in, mask_in), preferred_element_type=F32) + bias_col
-    act_value, slope = gelu_parts(pre_act)
-    hidden_out[0] = act_value.astype(BF16)
-    grad_hidden = jnp.dot(
-        wide(w_out), tall(grad, cols_out, mask_out), preferred_element_type=F32
-    )
-    grad_pre = grad_hidden * slope
-    low_out[0] = grad_pre.astype(BF16)
-    turned = jnp.transpose(grad_pre)
-    bias_out[pl.ds(where_row, 1), :] = jnp.sum(turned, axis=0, keepdims=True)
-    pieces = jnp.dot(turned.astype(BF16), w_wide, preferred_element_type=F32)
-    for s in range(slots):
-
-        @pl.when(mask_in[row, s] > 0)
-        def _():
-            total[cols_in[row, s]] += pieces[:, s * BLK : (s + 1) * BLK]
-
-    @pl.when(row == rows - 1)
+    def wide(ref, g):
+        return jnp.concatenate([ref[g, s] for s in range(slots)], axis=1)
+
+    several = range(group)
+    line = [step * group + g for g in several]
+    where_row = [stored[line[g]] for g in several]
+    pre_act = []
+    for g in several:
+        bias_row = bias_wide[pl.ds(where_row[g], 1), :]
+        bias_col = jnp.transpose(jnp.broadcast_to(bias_row, (BLK, BLK)))
+        pre_act.append(
+            jnp.dot(
+                wide(w_in, g), tall(act, meta, line[g], slots, 0), preferred_element_type=F32
+            )
+            + bias_col
+        )
+    grad_hidden = [
+        jnp.dot(
+            wide(w_out, g), tall(grad, meta, line[g], slots, 2 * slots), preferred_element_type=F32
+        )
+        for g in several
+    ]
+    turned = []
+    for g in several:
+        act_value, slope = gelu_parts(pre_act[g])
+        hidden_out[g] = act_value.astype(BF16)
+        grad_pre = grad_hidden[g] * slope
+        low_out[g] = grad_pre.astype(BF16)
+        turned.append(jnp.transpose(grad_pre))
+    pieces = [
+        jnp.dot(turned[g].astype(BF16), wide(w_in, g), preferred_element_type=F32) for g in several
+    ]
+    for g in several:
+        bias_out[pl.ds(where_row[g], 1), :] = jnp.sum(turned[g], axis=0, keepdims=True)
+        for s in range(slots):
+            piece = pieces[g][:, s * BLK : (s + 1) * BLK]
+            total[meta[s, line[g]]] += jnp.where(meta[slots + s, line[g]] > 0, piece, 0.0)
+
+    @pl.when(step == pl.num_programs(0) - 1)
     def _():
         chips = tensor // 2
         per = dblocks // tensor
@@ -143,11 +162,11 @@
 
 def scatter_kernel(
     tensor, sections, slots, rows, per,
-    cols_in, mask_in, cols_out, mask_out,
+    meta,
     part, bias_part, hidden, low, act, grad,
     tiles_in, tiles_out, bias_sum, handed,
-    held_in, held_out, from_pair, pair_sum, from_chips, final, bias_from, bias_keep,
-    pair_send, pair_recv, chip_send, chip_recv, bias_send, bias_recv, hand_send, hand_recv, store,
+    from_pair, pair_sum, from_chips, final, bias_from,
+    pair_send, pair_recv, chip_send, chip_recv, bias_send, bias_recv, hand_send, hand_recv,
 ):
     chips = tensor // 2
     me = lax.axis_index("tensor")
@@ -204,28 +223,17 @@
             device_id_type=MESH,
         )
 
-    def tall(ref, cols, mask, row):
-        return jnp.concatenate(
-            [
-                jnp.where(mask[row, s] > 0, ref[cols[row, s]], jnp.zeros((BLK, BLK), BF16))
-                for s in range(slots)
-            ],
-            axis=0,
-        )
-
     def out_product(left, right):
         return lax.dot_general(
             left, right, (((1,), (1,)), ((), ())), preferred_element_type=F32
         ).astype(BF16)
 
     def one_row(row, carry):
-        got_in = out_product(low[row], tall(act, cols_in, mask_in, row))
-        got_out = out_product(hidden[row], tall(grad, cols_out, mask_out, row))
+        got_in = out_product(low[row], tall(act, meta, row, slots, 0))
+        got_out = out_product(hidden[row], tall(grad, meta, row, slots, 2 * slots))
         for s in range(slots):
-            held_in[row, s] = got_in[:, s * BLK : (s + 1) * BLK]
-            held_out[row, s] = got_out[:, s * BLK : (s + 1) * BLK]
-        pltpu.make_async_copy(held_in.at[row], tiles_in.at[row], store.at[0]).start()
-        pltpu.make_async_copy(held_out.at[row], tiles_out.at[row], store.at[1]).start()
+            tiles_in[row, s] = got_in[:, s * BLK : (s + 1) * BLK]
+            tiles_out[row, s] = got_out[:, s * BLK : (s + 1) * BLK]
         return carry
 
     first, second = rows // 4, rows - rows // 4
@@ -264,13 +272,8 @@
     for step in range(1, tensor):
         bias_copy(step).wait()
         bias_total = bias_total + bias_from[step]
-    bias_keep[...] = bias_total
-    keep = pltpu.make_async_copy(bias_keep, bias_sum, store.at[2])
-    keep.start()
-    keep.wait()
+    bias_sum[...] = bias_total
     hand.wait()
-    pltpu.make_async_copy(held_in, tiles_in, store.at[0]).wait()
-    pltpu.make_async_copy(held_out, tiles_out, store.at[1]).wait()
 
 
 def local(
@@ -284,6 +287,8 @@
     per = depth // BLK
     dblocks = per * tensor
     hblocks = rows * tensor
+    group = 4 if rows % 4 == 0 else 1
+    meta = jnp.concatenate([cols_in[0].T, mask_in[0].T, cols_out[0].T, mask_out[0].T], axis=0)
     any_spec = pl.BlockSpec(memory_space=pl.ANY)
     vmem_spec = pl.BlockSpec(memory_space=pltpu.VMEM)
     smem_spec = pl.BlockSpec(memory_space=pltpu.SMEM)
@@ -297,9 +302,11 @@
             jax.ShapeDtypeStruct((tensor, rows, BLK), BF16),
         ),
         in_specs=[any_spec] * 3,
-        out_specs=[any_spec] * 3,
+        out_specs=[vmem_spec] * 3,
         scratch_shapes=[dma((3, chips))] * 4 + [dma((3,))],
-        compiler_params=pltpu.CompilerParams(collective_id=0, has_side_effects=True),
+        compiler_params=pltpu.CompilerParams(
+            collective_id=0, has_side_effects=True, vmem_limit_bytes=16 << 20
+        ),
         name="gather_inputs",
     )(
         activations.reshape(per, BLK, BLK),
@@ -312,10 +319,10 @@
     def whole(*shape):
         return pl.BlockSpec(shape, lambda row, *_: (0,) * len(shape))
 
-    tile_spec = pl.BlockSpec((1, slots, BLK, BLK), lambda row, *_: (row, 0, 0, 0))
-    block_spec = pl.BlockSpec((1, BLK, BLK), lambda row, *_: (row, 0, 0))
+    tile_spec = pl.BlockSpec((group, slots, BLK, BLK), lambda row, *_: (row, 0, 0, 0))
+    block_spec = pl.BlockSpec((group, BLK, BLK), lambda row, *_: (row, 0, 0))
     hidden, low, part, bias_part = pl.pallas_call(
-        functools.partial(row_kernel, slots, rows, dblocks, tensor),
+        functools.partial(row_kernel, slots, group, dblocks, tensor),
         out_shape=(
             jax.ShapeDtypeStruct((rows, BLK, BLK), BF16),
             jax.ShapeDtypeStruct((rows, BLK, BLK), BF16),
@@ -323,8 +330,8 @@
             jax.ShapeDtypeStruct((hblocks, BLK), F32),
         ),
         grid_spec=pltpu.PrefetchScalarGridSpec(
-            num_scalar_prefetch=5,
-            grid=(rows,),
+            num_scalar_prefetch=2,
+            grid=(rows // group,),
             in_specs=[
                 tile_spec,
                 tile_spec,
@@ -343,10 +350,10 @@
                 pltpu.VMEM((hblocks, BLK), F32),
             ],
         ),
-        compiler_params=pltpu.CompilerParams(vmem_limit_bytes=48 << 20),
+        compiler_params=pltpu.CompilerParams(vmem_limit_bytes=42 << 20),
         name="rows",
     )(
-        cols_in[0], mask_in[0], cols_out[0], mask_out[0], block_rows[0],
+        meta, block_rows[0],
         w_in[0], w_out[0], act_all, grad_all, bias_all,
     )
 
@@ -358,29 +365,25 @@
             jax.ShapeDtypeStruct((rows, BLK), F32),
             jax.ShapeDtypeStruct((per, BLK, BLK), BF16),
         ),
-        in_specs=[smem_spec] * 4 + [vmem_spec] * 6,
-        out_specs=[any_spec] * 4,
+        in_specs=[smem_spec] + [vmem_spec] * 6,
+        out_specs=[vmem_spec] * 4,
         scratch_shapes=[
-            pltpu.VMEM((rows, slots, BLK, BLK), BF16),
-            pltpu.VMEM((rows, slots, BLK, BLK), BF16),
             pltpu.VMEM((chips, per, BLK, BLK), BF16),
             pltpu.VMEM((chips, per, BLK, BLK), BF16),
             pltpu.VMEM((chips, per, BLK, BLK), BF16),
             pltpu.VMEM((per, BLK, BLK), BF16),
             pltpu.VMEM((tensor, rows, BLK), F32),
-            pltpu.VMEM((rows, BLK), F32),
             dma(()), dma(()),
             dma((chips,)), dma((chips,)),
             dma((tensor,)), dma((tensor,)),
             dma(()), dma(()),
-            dma((3,)),
         ],
         compiler_params=pltpu.CompilerParams(
-            collective_id=1, has_side_effects=True, vmem_limit_bytes=48 << 20
+            collective_id=1, has_side_effects=True, vmem_limit_bytes=16 << 20
         ),
         name="scatter_tiles",
     )(
-        cols_in[0], mask_in[0], cols_out[0], mask_out[0],
+        meta,
         part, bias_part.reshape(tensor, rows, BLK), hidden, low, act_all, grad_all,
     )
     return (

time: 109 us -> 81.1 us (0.74)
  Pallas kernels: 89.6 us -> 68.6 us
  local copies, waits for them, and re-layouts: 16.8 us -> 10.7 us
    pallas_call x1, Pallas kernels: 30.7 us -> 11.8 us  [local(): pl.pallas_call(functools.partial(row_kernel, slots, group, dblocks, tenso...]
    unnamed x14 -> x10, local copies, waits for them, and re-layouts: 16.8 us -> 9.26 us
    pallas_call x1, Pallas kernels: 28.5 us -> 27 us  [local(): pl.pallas_call(functools.partial(scatter_kernel, tensor, sections, slots,...]
    transpose x0 -> x2, local copies, waits for them, and re-layouts: none -> 1.42 us  [the longest x1 0.71 us: local(): mask_out[0]]
where the time goes in v2:
time: 81.1 us; the launch traced here: 80.7 us
  Pallas kernels  68.6 us (85%)
  local copies, waits for them, and re-layouts  10.7 us (13%)
    pallas_call x1, Pallas kernels, local(): pl.pallas_call(functools.partial(gather_kernel, tensor), out_shape=(jax.S...  29.7 us
    pallas_call x1, Pallas kernels, local(): pl.pallas_call(functools.partial(scatter_kernel, tensor, sections, slots,...  27 us
    pallas_call x1, Pallas kernels, local(): pl.pallas_call(functools.partial(row_kernel, slots, group, dblocks, tenso...  11.8 us
    unnamed x10, local copies, waits for them, and re-layouts  9.26 us

profile of v2, /device:TPU:0, one launch (start us, length us, event | category | flops | bytes accessed | tf_op | source)
XLA Modules:
  0.0 80.7 jit_solution(12357354709077890192)
XLA Ops:
  0.6 0.8 reduce
  1.4 0.7 copy_bitcast_fusion.2
  2.1 0.7 copy_bitcast_fusion
  2.8 0.0 copy-start
  2.8 0.9 %copy-done = bf16[1,1024,128]{2,1,0:T(8,128)(2,1)S(1)} copy-done((bf16[1,1024,128]{2,1,0:T(8,128)(2,1)S(1)}, bf16[1,1024,128]{2,1,0:T(8,128)(2,1)}, u32[]{:S(2)}) %copy-start) | copy-done | bytes 262168
  3.8 0.0 copy-start.1
  3.8 0.9 %copy-done.1 = bf16[1,1024,128]{2,1,0:T(8,128)(2,1)S(1)} copy-done((bf16[1,1024,128]{2,1,0:T(8,128)(2,1)S(1)}, bf16[1,1024,128]{2,1,0:T(8,128)(2,1)}, u32[]{:S(2)}) %copy-start.1) | copy-done | bytes 262168
  4.7 29.7 %gather_inputs.1 = (bf16[8,8,128,128]{3,2,1,0:T(8,128)(2,1)S(1)}, bf16[8,8,128,128]{3,2,1,0:T(8,128)(2,1)S(1)}, bf16[8,32,128]{2,1,0:T(8,128)(2,1)S(1)}) custom-call(bf16[8,128,128]{2,1,0:T(8,128)(2,1)S(1)} %bitcast.35, bf16[8,128,128]{2,1,0:T(8,128)(2,1)S(1)} %bitcast.36, bf16[32,128]{1,0:T(8,128)(2,1)S(1)} %bitcast.39), custom_call_target="tpu_custom_call" | custom-call | tf_op jit(solution)/shard_map/gather_inputs/pallas_call | solution.py:297
  34.4 0.0 copy-start.2
  34.4 0.6 copy-done.2
  35.1 11.8 %rows.1 = (bf16[32,128,128]{2,1,0:T(8,128)(2,1)S(1)}, bf16[32,128,128]{2,1,0:T(8,128)(2,1)S(1)}, bf16[2,4,8,128,128]{4,3,2,1,0:T(8,128)(2,1)S(1)}, f32[256,128]{1,0:T(8,128)S(1)}) custom-call(s32[24,32]{1,0:T(8,128)S(1)} %pad_add_fusion.meta, s32[32]{0:T(128)S(1)} %bitcast.41, bf16[32,6,128,128]{3,2,1,0:T(8,128)(2,1)} %bitcast.42, ...), custom_call_target="tpu_custom_call" | custom-call | tf_op jit(solution)/shard_map/rows/pallas_call | solution.py:324
  46.9 27.0 %scatter_tiles.1 = (bf16[32,6,128,128]{3,2,1,0:T(8,128)(2,1)S(1)}, bf16[32,6,128,128]{3,2,1,0:T(8,128)(2,1)S(1)}, f32[32,128]{1,0:T(8,128)S(1)}, bf16[8,128,128]{2,1,0:T(8,128)(2,1)S(1)}) custom-call(s32[24,32]{1,0:T(8,128)S(1)} %pad_add_fusion.meta, bf16[2,4,8,128,128]{4,3,2,1,0:T(8,128)(2,1)S(1)} %get-tuple-element.18.part, f32[8,32,128]{2,1,0:T(8,128)S(1)} %bitcast.38, ...), custom_call_target="tpu_custom_call" | custom-call | tf_op jit(solution)/shard_map/scatter_tiles/pallas_call | solution.py:360
  74.0 2.7 %copy.26 = bf16[1,32,6,128,128]{4,3,2,1,0:T(8,128)(2,1)} copy(bf16[1,32,6,128,128]{4,3,2,1,0:T(8,128)(2,1)S(1)} %bitcast.34) | data formatting | bytes 12582912
  76.7 2.7 %copy.27 = bf16[1,32,6,128,128]{4,3,2,1,0:T(8,128)(2,1)} copy(bf16[1,32,6,128,128]{4,3,2,1,0:T(8,128)(2,1)S(1)} %bitcast.33) | data formatting | bytes 12582912
  79.4 0.6 copy.28
  80.0 0.7 copy.29
  (1 shorter events, 0.0 us)
Async XLA Ops:
  2.8 1.0 %copy-start = (bf16[1,1024,128]{2,1,0:T(8,128)(2,1)S(1)}, bf16[1,1024,128]{2,1,0:T(8,128)(2,1)}, u32[]{:S(2)}) copy-start(bf16[1,1024,128]{2,1,0:T(8,128)(2,1)} %param.10) | copy-start | bytes 786436
  3.8 0.9 %copy-start.1 = (bf16[1,1024,128]{2,1,0:T(8,128)(2,1)S(1)}, bf16[1,1024,128]{2,1,0:T(8,128)(2,1)}, u32[]{:S(2)}) copy-start(bf16[1,1024,128]{2,1,0:T(8,128)(2,1)} %param.11) | copy-start | bytes 786436
  34.4 0.7 copy-start.2

commit v3 on v2

--- a/solution.py
+++ b/solution.py
@@ -63,23 +63,75 @@
             device_id_type=MESH,
         )
 
-    order = (2, 0, 1)
-    for kind in order:
+    everything = [(kind, step) for kind in (2, 0, 1) for step in range(1, chips)]
+    if chips == 4:
+        low_bit = lax.rem(chip, 2)
+        side = chip + 1 - 2 * low_bit
+        over = lax.rem(chip + 2, chips)
+        across = lax.rem(side + 2, chips)
+
+        def link(kind, step):
+            return pltpu.make_async_remote_copy(
+                src_ref=results[kind].at[(side, over)[kind] * 2 + core] if step == 3 else sources[kind],
+                dst_ref=results[kind].at[((side, over)[kind] * 2 + core) if step == 3 else me],
+                send_sem=send.at[kind, step],
+                recv_sem=recv.at[kind, step],
+                device_id=(sec, ((over, side)[kind] if step == 3 else (side, over)[step - 1]) * 2 + core),
+                device_id_type=MESH,
+            )
+
+        def pass_on(kind, step):
+            slot = (side, over, across)[step - 1] * 2 + core
+            return pltpu.make_async_remote_copy(
+                src_ref=results[kind].at[slot],
+                dst_ref=results[kind].at[slot],
+                send_sem=fsend.at[kind, step],
+                recv_sem=frecv.at[kind, step],
+                device_id=(sec, partner),
+                device_id_type=MESH,
+            )
+
+        first = [(0, 1), (1, 2), (1, 1), (0, 2)]
+        for kind, step in first:
+            link(kind, step).start()
         for step in range(1, chips):
+            far(2, step).start()
+        for kind in (0, 1, 2):
+            near(kind, 0).start()
+            pltpu.make_async_copy(sources[kind], results[kind].at[me], own.at[kind]).start()
+        for kind, step in first:
+            link(kind, step).wait_recv()
+            if step == kind + 1:
+                link(kind, 3).start()
+            pass_on(kind, step).start()
+        for step in range(1, chips):
+            far(2, step).wait_recv()
+            near(2, step).start()
+        for kind in (0, 1):
+            link(kind, 3).wait_recv()
+            pass_on(kind, 3).start()
+        for kind in (0, 1):
+            for step in range(1, chips):
+                link(kind, step).wait_send()
+                pass_on(kind, step).wait()
+        for step in range(1, chips):
+            far(2, step).wait_send()
+            near(2, step).wait()
+    else:
+        for kind, step in everything:
             far(kind, step).start()
-    for kind in order:
-        near(kind, 0).start()
-        pltpu.make_async_copy(sources[kind], results[kind].at[me], own.at[kind]).start()
-    for kind in order:
-        for step in range(1, chips):
+        for kind in (2, 0, 1):
+            near(kind, 0).start()
+            pltpu.make_async_copy(sources[kind], results[kind].at[me], own.at[kind]).start()
+        for kind, step in everything:
             far(kind, step).wait_recv()
             near(kind, step).start()
-    for kind in order:
+        for kind, step in everything:
+            far(kind, step).wait_send()
+            near(kind, step).wait()
+    for kind in (0, 1, 2):
         pltpu.make_async_copy(sources[kind], results[kind].at[me], own.at[kind]).wait()
-        for step in range(1, chips):
-            far(kind, step).wait_send()
-        for step in range(chips):
-            near(kind, step).wait()
+        near(kind, 0).wait()
 
 
 def tall(ref, meta, row, slots, first):
@@ -98,7 +150,7 @@
 
 def row_kernel(
     slots, group, dblocks, tensor,
-    meta, stored,
+    meta,
     w_in, w_out, act, grad, bias,
     hidden_out, low_out, part_out, bias_out,
     total, bias_wide,
@@ -117,7 +169,7 @@
 
     several = range(group)
     line = [step * group + g for g in several]
-    where_row = [stored[line[g]] for g in several]
+    where_row = [meta[4 * slots, line[g]] for g in several]
     pre_act = []
     for g in several:
         bias_row = bias_wide[pl.ds(where_row[g], 1), :]
@@ -161,7 +213,7 @@
 
 
 def scatter_kernel(
-    tensor, sections, slots, rows, per,
+    tensor, sections, slots, rows, per, parts,
     meta,
     part, bias_part, hidden, low, act, grad,
     tiles_in, tiles_out, bias_sum, handed,
@@ -189,15 +241,21 @@
         pl.semaphore_signal(barrier, inc=1, device_id=(section, me), device_id_type=MESH)
     pl.semaphore_wait(barrier, tensor + 1)
 
-    pair = pltpu.make_async_remote_copy(
-        src_ref=part.at[1 - core],
-        dst_ref=from_pair,
-        send_sem=pair_send,
-        recv_sem=pair_recv,
-        device_id=(sec, partner),
-        device_id_type=MESH,
-    )
-    pair.start()
+    size = per // parts
+
+    def pair(part_no):
+        blocks = pl.ds(part_no * size, size)
+        return pltpu.make_async_remote_copy(
+            src_ref=part.at[1 - core, :, blocks],
+            dst_ref=from_pair.at[:, blocks],
+            send_sem=pair_send.at[part_no],
+            recv_sem=pair_recv.at[part_no],
+            device_id=(sec, partner),
+            device_id_type=MESH,
+        )
+
+    for part_no in range(parts):
+        pair(part_no).start()
 
     def bias_copy(step):
         peer = lax.rem(me + step, tensor)
@@ -213,13 +271,25 @@
     for step in range(1, tensor):
         bias_copy(step).start()
 
-    def chip_copy(step):
-        return pltpu.make_async_remote_copy(
-            src_ref=pair_sum.at[step],
-            dst_ref=from_chips.at[step],
-            send_sem=chip_send.at[step],
-            recv_sem=chip_recv.at[step],
+    def chip_copy(part_no, step):
+        blocks = pl.ds(part_no * size, size)
+        return pltpu.make_async_remote_copy(
+            src_ref=pair_sum.at[step, blocks],
+            dst_ref=from_chips.at[step, blocks],
+            send_sem=chip_send.at[part_no, step],
+            recv_sem=chip_recv.at[part_no, step],
             device_id=(sec, ahead_chip(step) * 2 + core),
+            device_id_type=MESH,
+        )
+
+    def hand(part_no):
+        blocks = pl.ds(part_no * size, size)
+        return pltpu.make_async_remote_copy(
+            src_ref=final.at[blocks],
+            dst_ref=handed.at[blocks],
+            send_sem=hand_send.at[part_no],
+            recv_sem=hand_recv.at[part_no],
+            device_id=(before, me),
             device_id_type=MESH,
         )
 
@@ -236,44 +306,45 @@
             tiles_out[row, s] = got_out[:, s * BLK : (s + 1) * BLK]
         return carry
 
-    first, second = rows // 4, rows - rows // 4
-    lax.fori_loop(0, first, one_row, 0)
-
-    pair.wait()
-    for step in list(range(1, chips)) + [0]:
-        where_chip = ahead_chip(step)
-        pair_sum[step] = (
-            part[core, where_chip].astype(F32) + from_pair[where_chip].astype(F32)
-        ).astype(BF16)
-        if step:
-            chip_copy(step).start()
-
-    lax.fori_loop(first, second, one_row, 0)
-
-    result = pair_sum[0].astype(F32)
-    for step in range(1, chips):
-        chip_copy(step).wait()
-        result = result + from_chips[step].astype(F32)
-    for block in range(per):
-        final[block] = jnp.transpose(result[block]).astype(BF16)
-    hand = pltpu.make_async_remote_copy(
-        src_ref=final,
-        dst_ref=handed,
-        send_sem=hand_send,
-        recv_sem=hand_recv,
-        device_id=(before, me),
-        device_id_type=MESH,
-    )
-    hand.start()
-
-    lax.fori_loop(second, rows, one_row, 0)
+    marks = [0]
+
+    def compute_to(share):
+        goal = (rows * share) // 32
+        lax.fori_loop(marks[-1], goal, one_row, 0)
+        marks.append(goal)
+
+    for part_no in range(parts):
+        compute_to((part_no + 1) * 4 // parts)
+        pair(part_no).wait()
+        mine = slice(part_no * size, (part_no + 1) * size)
+        for step in list(range(1, chips)) + [0]:
+            where_chip = ahead_chip(step)
+            pair_sum[step, mine] = (
+                part[core, where_chip, mine].astype(F32) + from_pair[where_chip, mine].astype(F32)
+            ).astype(BF16)
+            if step:
+                chip_copy(part_no, step).start()
+
+    for part_no in range(parts):
+        compute_to(4 + (part_no + 1) * 24 // parts)
+        mine = slice(part_no * size, (part_no + 1) * size)
+        result = pair_sum[0, mine].astype(F32)
+        for step in range(1, chips):
+            chip_copy(part_no, step).wait()
+            result = result + from_chips[step, mine].astype(F32)
+        for block in range(size):
+            final[part_no * size + block] = jnp.transpose(result[block]).astype(BF16)
+        hand(part_no).start()
+
+    compute_to(32)
 
     bias_total = bias_part[me]
     for step in range(1, tensor):
         bias_copy(step).wait()
         bias_total = bias_total + bias_from[step]
     bias_sum[...] = bias_total
-    hand.wait()
+    for part_no in range(parts):
+        hand(part_no).wait()
 
 
 def local(
@@ -288,8 +359,10 @@
     dblocks = per * tensor
     hblocks = rows * tensor
     group = 4 if rows % 4 == 0 else 1
-    meta = jnp.concatenate([cols_in[0].T, mask_in[0].T, cols_out[0].T, mask_out[0].T], axis=0)
-    any_spec = pl.BlockSpec(memory_space=pl.ANY)
+    parts = 4 if per % 4 == 0 else 1
+    meta = jnp.concatenate(
+        [cols_in[0].T, mask_in[0].T, cols_out[0].T, mask_out[0].T, block_rows], axis=0
+    )
     vmem_spec = pl.BlockSpec(memory_space=pltpu.VMEM)
     smem_spec = pl.BlockSpec(memory_space=pltpu.SMEM)
     dma = pltpu.SemaphoreType.DMA
@@ -301,7 +374,7 @@
             jax.ShapeDtypeStruct((tensor, per, BLK, BLK), BF16),
             jax.ShapeDtypeStruct((tensor, rows, BLK), BF16),
         ),
-        in_specs=[any_spec] * 3,
+        in_specs=[pl.BlockSpec(memory_space=pltpu.HBM)] * 3,
         out_specs=[vmem_spec] * 3,
         scratch_shapes=[dma((3, chips))] * 4 + [dma((3,))],
         compiler_params=pltpu.CompilerParams(
@@ -330,7 +403,7 @@
             jax.ShapeDtypeStruct((hblocks, BLK), F32),
         ),
         grid_spec=pltpu.PrefetchScalarGridSpec(
-            num_scalar_prefetch=2,
+            num_scalar_prefetch=1,
             grid=(rows // group,),
             in_specs=[
                 tile_spec,
@@ -353,12 +426,12 @@
         compiler_params=pltpu.CompilerParams(vmem_limit_bytes=42 << 20),
         name="rows",
     )(
-        meta, block_rows[0],
+        meta,
         w_in[0], w_out[0], act_all, grad_all, bias_all,
     )
 
     tiles_in, tiles_out, bias_sum, handed = pl.pallas_call(
-        functools.partial(scatter_kernel, tensor, sections, slots, rows, per),
+        functools.partial(scatter_kernel, tensor, sections, slots, rows, per, parts),
         out_shape=(
             jax.ShapeDtypeStruct((rows, slots, BLK, BLK), BF16),
             jax.ShapeDtypeStruct((rows, slots, BLK, BLK), BF16),
@@ -373,10 +446,10 @@
             pltpu.VMEM((chips, per, BLK, BLK), BF16),
             pltpu.VMEM((per, BLK, BLK), BF16),
             pltpu.VMEM((tensor, rows, BLK), F32),
-            dma(()), dma(()),
-            dma((chips,)), dma((chips,)),
+            dma((parts,)), dma((parts,)),
+            dma((parts, chips)), dma((parts, chips)),
             dma((tensor,)), dma((tensor,)),
-            dma(()), dma(()),
+            dma((parts,)), dma((parts,)),
         ],
         compiler_params=pltpu.CompilerParams(
             collective_id=1, has_side_effects=True, vmem_limit_bytes=16 << 20

time: 81.1 us -> 70.9 us (0.87)
  Pallas kernels: 68.6 us -> 58.2 us
    pallas_call x1, Pallas kernels: 29.7 us -> 24.1 us  [local(): pl.pallas_call(functools.partial(gather_kernel, tensor), out_shape=(jax.S...]
    pallas_call x1, Pallas kernels: 27 us -> 22.2 us  [local(): pl.pallas_call(functools.partial(scatter_kernel, tensor, sections, slots,...]
    concatenate x0 -> x1, local copies, waits for them, and re-layouts: none -> 0.81 us  [local(): jnp.concatenate([cols_in[0].T, mask_in[0].T, cols_out[0].T, mask_out[0].T...]
    unnamed x10 -> x8, local copies, waits for them, and re-layouts: 9.26 us -> 8.61 us
where the time goes in v3:
time: 70.9 us; the launch traced here: 70.5 us
  Pallas kernels  58.2 us (82%)
  local copies, waits for them, and re-layouts  10.8 us (15%)
  other arithmetic  0.77 us (1%)
    pallas_call x1, Pallas kernels, local(): pl.pallas_call(functools.partial(gather_kernel, tensor), out_shape=(jax.S...  24.1 us
    pallas_call x1, Pallas kernels, local(): pl.pallas_call(functools.partial(scatter_kernel, tensor, sections, slots,...  22.2 us
    pallas_call x1, Pallas kernels, local(): pl.pallas_call(functools.partial(row_kernel, slots, group, dblocks, tenso...  11.9 us
    unnamed x8, local copies, waits for them, and re-layouts  8.61 us

profile of v3, /device:TPU:0, one launch (start us, length us, event | category | flops | bytes accessed | tf_op | source)
XLA Modules:
  0.0 70.5 jit_solution(4179728092308291015)
XLA Ops:
  0.6 0.8 %reduce = bf16[4096]{0:T(1024)(128)(2,1)S(1)} reduce(bf16[1,4096]{1,0:T(2,128)(2,1)} %param.14, bf16[]{:T(256)} %constant.10), dimensions={0}, to_apply=%param.14.reduce_sub_computation | reduce | bytes 16386 | tf_op args[4]
  1.4 0.7 copy_bitcast_fusion.2
  2.1 0.7 %copy_bitcast_fusion = (s32[6,32]{1,0:T(8,128)S(1)}, s32[6,32]{1,0:T(8,128)S(1)}) fusion(s32[1,32,6]{1,0,2:T(1,128)} %param.18, s32[1,32,6]{1,0,2:T(1,128)} %param.17), kind=kLoop, calls=%fused_computation | loop fusion | bytes 3072 | tf_op jit(solution)/shard_map/transpose | solution.py:364
  2.8 0.8 %concatenate.3.meta = s32[25,32]{1,0:T(8,128)S(1)} concatenate(s32[6,32]{1,0:T(8,128)S(1)} %get-tuple-element.29, s32[6,32]{1,0:T(8,128)S(1)} %get-tuple-element.28, s32[6,32]{1,0:T(8,128)S(1)} %get-tuple-element.27, s32[6,32]{1,0:T(8,128)S(1)} %get-tuple-element.26, s32[1,32]{1,0:T(1,128)} %param.19), dimensions={0} | concatenate | bytes 6400 | tf_op jit(solution)/shard_map/concatenate | solution.py:363
  3.6 0.0 copy-start
  3.6 0.9 %copy-done = bf16[1,1024,128]{2,1,0:T(8,128)(2,1)S(1)} copy-done((bf16[1,1024,128]{2,1,0:T(8,128)(2,1)S(1)}, bf16[1,1024,128]{2,1,0:T(8,128)(2,1)}, u32[]{:S(2)}) %copy-start) | copy-done | bytes 262168
  4.6 0.0 copy-start.1
  4.6 0.9 %copy-done.1 = bf16[1,1024,128]{2,1,0:T(8,128)(2,1)S(1)} copy-done((bf16[1,1024,128]{2,1,0:T(8,128)(2,1)S(1)}, bf16[1,1024,128]{2,1,0:T(8,128)(2,1)}, u32[]{:S(2)}) %copy-start.1) | copy-done | bytes 262168
  5.5 24.1 %gather_inputs.1 = (bf16[8,8,128,128]{3,2,1,0:T(8,128)(2,1)S(1)}, bf16[8,8,128,128]{3,2,1,0:T(8,128)(2,1)S(1)}, bf16[8,32,128]{2,1,0:T(8,128)(2,1)S(1)}) custom-call(bf16[8,128,128]{2,1,0:T(8,128)(2,1)S(1)} %bitcast.34, bf16[8,128,128]{2,1,0:T(8,128)(2,1)S(1)} %bitcast.35, bf16[32,128]{1,0:T(8,128)(2,1)S(1)} %bitcast.38), custom_call_target="tpu_custom_call" | custom-call | tf_op jit(solution)/shard_map/gather_inputs/pallas_call | solution.py:370
  29.6 11.9 %rows.1 = (bf16[32,128,128]{2,1,0:T(8,128)(2,1)S(1)}, bf16[32,128,128]{2,1,0:T(8,128)(2,1)S(1)}, bf16[2,4,8,128,128]{4,3,2,1,0:T(8,128)(2,1)S(1)}, f32[256,128]{1,0:T(8,128)S(1)}) custom-call(s32[25,32]{1,0:T(8,128)S(1)} %concatenate.3.meta, bf16[32,6,128,128]{3,2,1,0:T(8,128)(2,1)} %bitcast.40, bf16[32,6,128,128]{3,2,1,0:T(8,128)(2,1)} %bitcast.41, ...), custom_call_target="tpu_custom_call" | custom-call | tf_op jit(solution)/shard_map/rows/pallas_call | solution.py:397
  41.5 22.2 %scatter_tiles.1 = (bf16[32,6,128,128]{3,2,1,0:T(8,128)(2,1)S(1)}, bf16[32,6,128,128]{3,2,1,0:T(8,128)(2,1)S(1)}, f32[32,128]{1,0:T(8,128)S(1)}, bf16[8,128,128]{2,1,0:T(8,128)(2,1)S(1)}) custom-call(s32[25,32]{1,0:T(8,128)S(1)} %concatenate.3.meta, bf16[2,4,8,128,128]{4,3,2,1,0:T(8,128)(2,1)S(1)} %get-tuple-element.18.part, f32[8,32,128]{2,1,0:T(8,128)S(1)} %bitcast.37, ...), custom_call_target="tpu_custom_call" | custom-call | tf_op jit(solution)/shard_map/scatter_tiles/pallas_call | solution.py:433
  63.8 2.7 %copy.26 = bf16[1,32,6,128,128]{4,3,2,1,0:T(8,128)(2,1)} copy(bf16[1,32,6,128,128]{4,3,2,1,0:T(8,128)(2,1)S(1)} %bitcast.33) | data formatting | bytes 12582912
  66.5 2.7 %copy.27 = bf16[1,32,6,128,128]{4,3,2,1,0:T(8,128)(2,1)} copy(bf16[1,32,6,128,128]{4,3,2,1,0:T(8,128)(2,1)S(1)} %bitcast.32) | data formatting | bytes 12582912
  69.2 0.6 copy.28
  69.8 0.7 copy.29
Async XLA Ops:
  3.6 0.9 %copy-start = (bf16[1,1024,128]{2,1,0:T(8,128)(2,1)S(1)}, bf16[1,1024,128]{2,1,0:T(8,128)(2,1)}, u32[]{:S(2)}) copy-start(bf16[1,1024,128]{2,1,0:T(8,128)(2,1)} %param.10) | copy-start | bytes 786436
  4.6 0.9 %copy-start.1 = (bf16[1,1024,128]{2,1,0:T(8,128)(2,1)S(1)}, bf16[1,1024,128]{2,1,0:T(8,128)(2,1)}, u32[]{:S(2)}) copy-start(bf16[1,1024,128]{2,1,0:T(8,128)(2,1)} %param.11) | copy-start | bytes 786436

commit v4 on v3

--- a/solution.py
+++ b/solution.py
@@ -134,12 +134,12 @@
         near(kind, 0).wait()
 
 
-def tall(ref, meta, row, slots, first):
+def tall(ref, cols, mask, row, slots):
     return jnp.concatenate(
         [
             jnp.where(
-                meta[first + slots + s, row] > 0,
-                ref[meta[first + s, row]],
+                mask[s, 0, row] > 0,
+                ref[cols[s, 0, row]],
                 jnp.zeros((BLK, BLK), BF16),
             )
             for s in range(slots)
@@ -150,7 +150,7 @@
 
 def row_kernel(
     slots, group, dblocks, tensor,
-    meta,
+    cols_in, mask_in, cols_out, mask_out, stored,
     w_in, w_out, act, grad, bias,
     hidden_out, low_out, part_out, bias_out,
     total, bias_wide,
@@ -169,20 +169,20 @@
 
     several = range(group)
     line = [step * group + g for g in several]
-    where_row = [meta[4 * slots, line[g]] for g in several]
+    where_row = [stored[0, line[g]] for g in several]
     pre_act = []
     for g in several:
         bias_row = bias_wide[pl.ds(where_row[g], 1), :]
         bias_col = jnp.transpose(jnp.broadcast_to(bias_row, (BLK, BLK)))
         pre_act.append(
             jnp.dot(
-                wide(w_in, g), tall(act, meta, line[g], slots, 0), preferred_element_type=F32
+                wide(w_in, g), tall(act, cols_in, mask_in, line[g], slots), preferred_element_type=F32
             )
             + bias_col
         )
     grad_hidden = [
         jnp.dot(
-            wide(w_out, g), tall(grad, meta, line[g], slots, 2 * slots), preferred_element_type=F32
+            wide(w_out, g), tall(grad, cols_out, mask_out, line[g], slots), preferred_element_type=F32
         )
         for g in several
     ]
@@ -200,7 +200,7 @@
         bias_out[pl.ds(where_row[g], 1), :] = jnp.sum(turned[g], axis=0, keepdims=True)
         for s in range(slots):
             piece = pieces[g][:, s * BLK : (s + 1) * BLK]
-            total[meta[s, line[g]]] += jnp.where(meta[slots + s, line[g]] > 0, piece, 0.0)
+            total[cols_in[s, 0, line[g]]] += jnp.where(mask_in[s, 0, line[g]] > 0, piece, 0.0)
 
     @pl.when(step == pl.num_programs(0) - 1)
     def _():
@@ -214,7 +214,7 @@
 
 def scatter_kernel(
     tensor, sections, slots, rows, per, parts,
-    meta,
+    cols_in, mask_in, cols_out, mask_out,
     part, bias_part, hidden, low, act, grad,
     tiles_in, tiles_out, bias_sum, handed,
     from_pair, pair_sum, from_chips, final, bias_from,
@@ -299,8 +299,8 @@
         ).astype(BF16)
 
     def one_row(row, carry):
-        got_in = out_product(low[row], tall(act, meta, row, slots, 0))
-        got_out = out_product(hidden[row], tall(grad, meta, row, slots, 2 * slots))
+        got_in = out_product(low[row], tall(act, cols_in, mask_in, row, slots))
+        got_out = out_product(hidden[row], tall(grad, cols_out, mask_out, row, slots))
         for s in range(slots):
             tiles_in[row, s] = got_in[:, s * BLK : (s + 1) * BLK]
             tiles_out[row, s] = got_out[:, s * BLK : (s + 1) * BLK]
@@ -347,6 +347,15 @@
         hand(part_no).wait()
 
 
+def write_kernel(*refs):
+    done = refs[8]
+    copies = [pltpu.make_async_copy(refs[i], refs[4 + i], done.at[i]) for i in range(4)]
+    for copy in copies:
+        copy.start()
+    for copy in copies:
+        copy.wait()
+
+
 def local(
     activations, out_grads, w_in, w_out, bias_in, cols_in, mask_in, cols_out, mask_out, block_rows
 ):
@@ -358,11 +367,11 @@
     per = depth // BLK
     dblocks = per * tensor
     hblocks = rows * tensor
-    group = 4 if rows % 4 == 0 else 1
+    group = next(each for each in (8, 4, 1) if rows % each == 0)
     parts = 4 if per % 4 == 0 else 1
-    meta = jnp.concatenate(
-        [cols_in[0].T, mask_in[0].T, cols_out[0].T, mask_out[0].T, block_rows], axis=0
-    )
+    tables = [jnp.transpose(each, (2, 0, 1)) for each in (cols_in, mask_in, cols_out, mask_out)]
+    tables = [pltpu.with_memory_space_constraint(each, pltpu.HBM) for each in tables]
+    block_rows = pltpu.with_memory_space_constraint(block_rows, pltpu.HBM)
     vmem_spec = pl.BlockSpec(memory_space=pltpu.VMEM)
     smem_spec = pl.BlockSpec(memory_space=pltpu.SMEM)
     dma = pltpu.SemaphoreType.DMA
@@ -382,8 +391,8 @@
         ),
         name="gather_inputs",
     )(
-        activations.reshape(per, BLK, BLK),
-        out_grads.reshape(per, BLK, BLK),
+        pltpu.with_memory_space_constraint(activations.reshape(per, BLK, BLK), pltpu.HBM),
+        pltpu.with_memory_space_constraint(out_grads.reshape(per, BLK, BLK), pltpu.HBM),
         bias_in.reshape(rows, BLK),
     )
     act_all = act_all.reshape(dblocks, BLK, BLK)
@@ -403,7 +412,7 @@
             jax.ShapeDtypeStruct((hblocks, BLK), F32),
         ),
         grid_spec=pltpu.PrefetchScalarGridSpec(
-            num_scalar_prefetch=1,
+            num_scalar_prefetch=5,
             grid=(rows // group,),
             in_specs=[
                 tile_spec,
@@ -426,7 +435,7 @@
         compiler_params=pltpu.CompilerParams(vmem_limit_bytes=42 << 20),
         name="rows",
     )(
-        meta,
+        *tables, block_rows,
         w_in[0], w_out[0], act_all, grad_all, bias_all,
     )
 
@@ -438,7 +447,7 @@
             jax.ShapeDtypeStruct((rows, BLK), F32),
             jax.ShapeDtypeStruct((per, BLK, BLK), BF16),
         ),
-        in_specs=[smem_spec] + [vmem_spec] * 6,
+        in_specs=[smem_spec] * 4 + [vmem_spec] * 6,
         out_specs=[vmem_spec] * 4,
         scratch_shapes=[
             pltpu.VMEM((chips, per, BLK, BLK), BF16),
@@ -456,9 +465,22 @@
         ),
         name="scatter_tiles",
     )(
-        meta,
+        *tables,
         part, bias_part.reshape(tensor, rows, BLK), hidden, low, act_all, grad_all,
     )
+    hbm_spec = pl.BlockSpec(memory_space=pl.ANY)
+    tiles_in, tiles_out, bias_sum, handed = pl.pallas_call(
+        write_kernel,
+        out_shape=[
+            jax.ShapeDtypeStruct(each.shape, each.dtype)
+            for each in (tiles_in, tiles_out, bias_sum, handed)
+        ],
+        in_specs=[vmem_spec] * 4,
+        out_specs=[hbm_spec] * 4,
+        scratch_shapes=[dma((4,))],
+        compiler_params=pltpu.CompilerParams(vmem_limit_bytes=16 << 20),
+        name="write_results",
+    )(tiles_in, tiles_out, bias_sum, handed)
     return (
         tiles_in[None],
         tiles_out[None],

time: 70.9 us -> 63.3 us (0.89)
  local copies, waits for them, and re-layouts: 10.8 us -> 0 us
  Pallas kernels: 58.2 us -> 61.6 us
    unnamed x8 -> x0, local copies, waits for them, and re-layouts: 8.61 us -> none
    pallas_call x0 -> x1, Pallas kernels: none -> 4.81 us  [local(): pl.pallas_call(write_kernel, out_shape=[jax.ShapeDtypeStruct(each.shape,...]
    pallas_call x1, Pallas kernels: 11.9 us -> 10.2 us  [local(): pl.pallas_call(functools.partial(row_kernel, slots, group, dblocks, tenso...]
    transpose x2 -> x0, local copies, waits for them, and re-layouts: 1.42 us -> none  [the longest x1 0.71 us: local(): mask_out[0]]
    concatenate x1 -> x0, local copies, waits for them, and re-layouts: 0.81 us -> none  [local(): jnp.concatenate([cols_in[0].T, mask_in[0].T, cols_out[0].T, mask_out[0].T...]
where the time goes in v4:
time: 63.3 us; the launch traced here: 63 us
  Pallas kernels  61.6 us (97%)
  other arithmetic  0.77 us (1%)
  between operations  0.65 us (1%)
    pallas_call x1, Pallas kernels, local(): pl.pallas_call(functools.partial(gather_kernel, tensor), out_shape=(jax.S...  24.3 us
    pallas_call x1, Pallas kernels, local(): pl.pallas_call(functools.partial(scatter_kernel, tensor, sections, slots,...  22.2 us
    pallas_call x1, Pallas kernels, local(): pl.pallas_call(functools.partial(row_kernel, slots, group, dblocks, tenso...  10.2 us
    pallas_call x1, Pallas kernels, local(): pl.pallas_call(write_kernel, out_shape=[jax.ShapeDtypeStruct(each.shape,...  4.81 us

profile of v4, /device:TPU:0, one launch (start us, length us, event | category | flops | bytes accessed | tf_op | source)
XLA Modules:
  0.0 63.0 jit_solution(15741352597913747250)
XLA Ops:
  0.6 0.8 %reduce = bf16[4096]{0:T(1024)(128)(2,1)S(1)} reduce(bf16[1,4096]{1,0:T(2,128)(2,1)} %param.14, bf16[]{:T(256)} %constant.10), dimensions={0}, to_apply=%param.14.reduce_sub_computation | reduce | bytes 16386 | tf_op args[4]
  1.4 24.3 %gather_inputs.1 = (bf16[8,8,128,128]{3,2,1,0:T(8,128)(2,1)S(1)}, bf16[8,8,128,128]{3,2,1,0:T(8,128)(2,1)S(1)}, bf16[8,32,128]{2,1,0:T(8,128)(2,1)S(1)}) custom-call(bf16[8,128,128]{2,1,0:T(8,128)(2,1)} %bitcast.24, bf16[8,128,128]{2,1,0:T(8,128)(2,1)} %bitcast.25, bf16[32,128]{1,0:T(8,128)(2,1)S(1)} %bitcast.21), custom_call_target="tpu_custom_call" | custom-call | tf_op jit(solution)/shard_map/gather_inputs/pallas_call | solution.py:379
  25.7 10.2 %rows.1 = (bf16[32,128,128]{2,1,0:T(8,128)(2,1)S(1)}, bf16[32,128,128]{2,1,0:T(8,128)(2,1)S(1)}, bf16[2,4,8,128,128]{4,3,2,1,0:T(8,128)(2,1)S(1)}, f32[256,128]{1,0:T(8,128)S(1)}) custom-call(s32[6,1,32]{2,1,0:T(1,128)} %bitcast.26, s32[6,1,32]{2,1,0:T(1,128)} %bitcast.28, s32[6,1,32]{2,1,0:T(1,128)} %bitcast.30, s32[6,1,32]{2,1,0:T(1,128)} %bitcast.32, ...), custom_call_target="tpu_custom_call" | custom-call | tf_op jit(solution)/shard_map/rows/pallas_call | solution.py:406
  36.0 22.2 %scatter_tiles.1 = (bf16[32,6,128,128]{3,2,1,0:T(8,128)(2,1)S(1)}, bf16[32,6,128,128]{3,2,1,0:T(8,128)(2,1)S(1)}, f32[32,128]{1,0:T(8,128)S(1)}, bf16[8,128,128]{2,1,0:T(8,128)(2,1)S(1)}) custom-call(s32[6,1,32]{2,1,0:T(1,128)} %bitcast.27, s32[6,1,32]{2,1,0:T(1,128)} %bitcast.29, s32[6,1,32]{2,1,0:T(1,128)} %bitcast.31, s32[6,1,32]{2,1,0:T(1,128)} %bitcast.33, ...), custom_call_target="tpu_custom_call" | custom-call | tf_op jit(solution)/shard_map/scatter_tiles/pallas_call | solution.py:442
  58.2 4.8 %write_results.1 = (bf16[32,6,128,128]{3,2,1,0:T(8,128)(2,1)}, bf16[32,6,128,128]{3,2,1,0:T(8,128)(2,1)}, f32[32,128]{1,0:T(8,128)}, bf16[8,128,128]{2,1,0:T(8,128)(2,1)}) custom-call(bf16[32,6,128,128]{3,2,1,0:T(8,128)(2,1)S(1)} %get-tuple-element.26.refs_0_, bf16[32,6,128,128]{3,2,1,0:T(8,128)(2,1)S(1)} %get-tuple-element.27.refs_1_, ...), custom_call_target="tpu_custom_call" | custom-call | tf_op jit(solution)/shard_map/write_results/pallas_call | solution.py:472
